TPU v7x, 32 devices: a whole 2x2x4 slice. The times are simulated.
32 devices in a mesh: row: 4 (over x, core), col: 8 (over z, y).
Axes of the slice: x: 2, y: 2, z: 4, core: 2. Of those that a mesh axis runs over, the one named last changes fastest.
Arguments:
- masters: float32 [128, 4096], P('col'), may hold values from -6 to 6
- inst_master: int32 [64, 128], P('row', 'col'), may hold values from 0 to 127
- inst_orient: int32 [64, 128], P('row', 'col'), may hold values from 0 to 3
- owner_map: int32 [128], replicated, may hold values from 0 to 127, each once
- tile_free: float32 [4096, 8192], P('row', 'col'), may hold values from -3 to 3
- target: float32 [4096, 8192], P('row', 'col'), may hold values from 0 to 1
- kernel_spectra: float32 [2, 128, 8, 128], replicated, may hold values from -6 to 6
- socs_weights: float32 [8], replicated, may hold values from 0.05 to 1
Outputs:
- resist: float32 [4096, 8192], P('row', 'col')
- new_mask: float32 [4096, 8192], P('row', 'col')
- masters_out: float32 [128, 4096], P('col')
Inputs may be any that keep to these rules, and one draw needn't show every extreme that they name: `inst_orient`: bit 0 reverses a cell's rows, bit 1 its columns. `owner_map`: each storage row is used by exactly one master; storage row r lies on index r // 16 of col.
All inputs are finite; a program needn't handle non-finite values.
Results may differ from a plain program's by a relative error of at most 0.0092.
Values may be sent and summed in bfloat16 or wider, within the bound.
A program may use at most 128 MiB of HBM per device.

v0:
```python
import math

import jax
import jax.numpy as jnp
from jax import lax
from jax.sharding import PartitionSpec as P

TILE = 512
TPD = 2
HALO = 64
CELL = 64


step_free = 1.0
step_master = 0.05
resist_gain = 2.0
resist_level = 1.8


def padded_2(value, sides, width):
    for axis, dim in sides:
        peers, length = (lax.axis_size(axis), value.shape[dim])
        up = [(i, (i + 1) % peers) for i in range(peers - 1)]
        down = [(j, i) for i, j in up]
        last = lax.slice_in_dim(value, length - width, length, axis=dim)
        initial = lax.slice_in_dim(value, 0, width, axis=dim)
        before = lax.ppermute(last, axis, up)
        after = lax.ppermute(initial, axis, down)
        value = jnp.concatenate([before, value, after], axis=dim)
    return value


def dot_plain(left, right):
    return jnp.dot(left, right, preferred_element_type=jnp.float32)


def dot_right_t(left, right):
    return lax.dot_general(
        left, right, (((1,), (1,)), ((), ())), preferred_element_type=jnp.float32
    )


def dot_left_t(left, right):
    return lax.dot_general(
        left, right, (((0,), (0,)), ((), ())), preferred_element_type=jnp.float32
    )


def tables(pad_side, band_side):
    freqs = jnp.arange(band_side, dtype=jnp.int32) - band_side // 2
    pixels = jnp.arange(pad_side, dtype=jnp.int32)
    phases = freqs[:, None] * pixels[None, :] % pad_side
    angles = phases.astype(jnp.float32) * (2.0 * math.pi / pad_side)
    return (jnp.cos(angles).astype(jnp.bfloat16), jnp.sin(angles).astype(jnp.bfloat16))


def tile_step(padded, target, spectra, weights, halo_side):
    pad_side = padded.shape[0]
    band_side = spectra.shape[1]
    kernels = spectra.shape[2]
    tile_side = pad_side - 2 * halo_side
    cos_full, sin_full = tables(pad_side, band_side)
    cos_in = cos_full[:, halo_side : halo_side + tile_side]
    sin_in = sin_full[:, halo_side : halo_side + tile_side]
    forw_re = dot_plain(cos_full, padded).astype(jnp.bfloat16)
    forw_im = (-dot_plain(sin_full, padded)).astype(jnp.bfloat16)
    spec_re = (dot_right_t(forw_re, cos_full) - dot_right_t(forw_im, sin_full)) / pad_side
    spec_im = (-dot_right_t(forw_re, sin_full) - dot_right_t(forw_im, cos_full)) / pad_side
    kern_re = spectra[0]
    kern_im = spectra[1]
    amp_re = (kern_re * spec_re[:, None, :] - kern_im * spec_im[:, None, :]).astype(jnp.bfloat16)
    amp_im = (kern_re * spec_im[:, None, :] + kern_im * spec_re[:, None, :]).astype(jnp.bfloat16)
    amp_re = amp_re.reshape(band_side, kernels * band_side)
    amp_im = amp_im.reshape(band_side, kernels * band_side)
    half_re = (dot_left_t(cos_in, amp_re) - dot_left_t(sin_in, amp_im)).astype(jnp.bfloat16)
    half_im = (dot_left_t(cos_in, amp_im) + dot_left_t(sin_in, amp_re)).astype(jnp.bfloat16)
    half_re = half_re.reshape(tile_side * kernels, band_side)
    half_im = half_im.reshape(tile_side * kernels, band_side)
    field_re = (dot_plain(half_re, cos_in) - dot_plain(half_im, sin_in)) / band_side
    field_im = (dot_plain(half_re, sin_in) + dot_plain(half_im, cos_in)) / band_side
    field_re = field_re.reshape(tile_side, kernels, tile_side)
    field_im = field_im.reshape(tile_side, kernels, tile_side)
    scaled = weights[None, :, None]
    intensity = jnp.sum(scaled * (field_re * field_re + field_im * field_im), axis=1)
    resist = jax.nn.sigmoid(resist_gain * (intensity - resist_level))
    slopes = 2.0 * (resist - target) * resist_gain * resist * (1.0 - resist)
    back_re = (2.0 / band_side * scaled * slopes[:, None, :] * field_re).astype(jnp.bfloat16)
    back_im = (2.0 / band_side * scaled * slopes[:, None, :] * field_im).astype(jnp.bfloat16)
    back_re = back_re.reshape(tile_side * kernels, tile_side)
    back_im = back_im.reshape(tile_side * kernels, tile_side)
    bhalf_re = (dot_right_t(back_re, cos_in) + dot_right_t(back_im, sin_in)).astype(jnp.bfloat16)
    bhalf_im = (dot_right_t(back_im, cos_in) - dot_right_t(back_re, sin_in)).astype(jnp.bfloat16)
    bhalf_re = bhalf_re.reshape(tile_side, kernels * band_side)
    bhalf_im = bhalf_im.reshape(tile_side, kernels * band_side)
    bamp_re = (dot_plain(cos_in, bhalf_re) + dot_plain(sin_in, bhalf_im)).reshape(
        band_side, kernels, band_side
    )
    bamp_im = (dot_plain(cos_in, bhalf_im) - dot_plain(sin_in, bhalf_re)).reshape(
        band_side, kernels, band_side
    )
    bspec_re = (jnp.sum(kern_re * bamp_re + kern_im * bamp_im, axis=1) / pad_side).astype(
        jnp.bfloat16
    )
    bspec_im = (jnp.sum(kern_re * bamp_im - kern_im * bamp_re, axis=1) / pad_side).astype(
        jnp.bfloat16
    )
    bforw_re = (dot_plain(bspec_re, cos_in) - dot_plain(bspec_im, sin_in)).astype(jnp.bfloat16)
    bforw_im = (-dot_plain(bspec_re, sin_in) - dot_plain(bspec_im, cos_in)).astype(jnp.bfloat16)
    gradient = dot_left_t(cos_in, bforw_re) - dot_left_t(sin_in, bforw_im)
    return (resist, gradient)


def orient_cells(cells, orient):
    flip_first = orient % 2 == 1
    flip_second = orient // 2 == 1
    cells = jnp.where(flip_first[..., None, None], cells[..., ::-1, :], cells)
    cells = jnp.where(flip_second[..., None, None], cells[..., :, ::-1], cells)
    return cells


def assemble(master_rows, slots, orient, cell_side):
    grid_rows, grid_cols = slots.shape
    cells = jnp.take(master_rows, slots.reshape(-1), axis=0)
    cells = cells.reshape(grid_rows, grid_cols, cell_side, cell_side)
    cells = orient_cells(cells, orient)
    return cells.transpose(0, 2, 1, 3).reshape(grid_rows * cell_side, grid_cols * cell_side)


def cells_of(image, orient, cell_side):
    grid_rows, grid_cols = orient.shape
    cells = image.reshape(grid_rows, cell_side, grid_cols, cell_side).transpose(0, 2, 1, 3)
    cells = orient_cells(cells, orient)
    return cells.reshape(grid_rows * grid_cols, cell_side * cell_side)


def smooth(master_rows, cell_side):
    grids = master_rows.reshape(-1, cell_side, cell_side)
    framed = jnp.pad(grids, ((0, 0), (1, 1), (1, 1)))
    beside_all = (
        framed[:, 2:, 1:-1] + framed[:, :-2, 1:-1] + framed[:, 1:-1, 2:] + framed[:, 1:-1, :-2]
    )
    return (0.5 * grids + 0.125 * beside_all).reshape(master_rows.shape)


def stitch_local(tiles):
    return tiles.reshape(TPD, TPD, TILE, TILE).transpose(0, 2, 1, 3).reshape(TPD * TILE, TPD * TILE)


def per_device(
    masters, inst_master, inst_orient, owner_map, tile_free, target, kernel_spectra, socs_weights
):
    stored = masters.shape[0]
    everything = lax.all_gather(masters, "col", axis=0, tiled=True)
    total_masters = everything.shape[0]
    matches = inst_master[..., None] == jnp.arange(total_masters, dtype=jnp.int32)
    slots = jnp.sum(jnp.where(matches, owner_map, 0), axis=-1)
    flat_slots = slots.reshape(-1)
    col_index = lax.axis_index("col")
    free_field = tile_free
    pad_side = TILE + 2 * HALO
    shading = jnp.tanh(assemble(everything, slots, inst_orient, CELL) + free_field)
    mask_block = shading.astype(jnp.bfloat16)
    padded = padded_2(mask_block, (("row", 0), ("col", 1)), HALO)

    def one_tile(tile_index):
        row_at = tile_index // TPD
        col_at = tile_index % TPD
        window = lax.dynamic_slice(padded, (row_at * TILE, col_at * TILE), (pad_side, pad_side))
        goal_tile = lax.dynamic_slice(target, (row_at * TILE, col_at * TILE), (TILE, TILE))
        return tile_step(window, goal_tile, kernel_spectra, socs_weights, HALO)

    resist_tiles, grad_tiles = lax.map(one_tile, jnp.arange(TPD * TPD, dtype=jnp.int32))
    resist = stitch_local(resist_tiles)
    grad_param = stitch_local(grad_tiles) * (1.0 - shading * shading)
    free_field = free_field - step_free * grad_param
    cell_grads = cells_of(grad_param, inst_orient, CELL)
    wanted = jnp.arange(total_masters, dtype=jnp.int32)
    selector = (flat_slots[None, :] == wanted[:, None]).astype(jnp.float32)
    whole_sum = lax.psum(
        jnp.dot(
            selector,
            cell_grads,
            precision=lax.Precision.HIGHEST,
            preferred_element_type=jnp.float32,
        ).astype(jnp.bfloat16),
        "row",
    )
    summed = lax.psum_scatter(whole_sum, "col", scatter_dimension=0, tiled=True).astype(jnp.float32)
    own_rows = lax.dynamic_slice_in_dim(everything, col_index * stored, stored, 0)
    fresh = smooth(own_rows - step_master * summed, CELL)
    everything = lax.all_gather(fresh.astype(jnp.bfloat16), "col", axis=0, tiled=True).astype(
        fresh.dtype
    )
    new_mask = jnp.tanh(assemble(everything, slots, inst_orient, CELL) + free_field)
    masters_out = lax.dynamic_slice_in_dim(everything, col_index * stored, stored, 0)
    return (resist, new_mask, masters_out)


def solution(mesh):
    in_specs = (
        P("col", None),
        P("row", "col"),
        P("row", "col"),
        P(),
        P("row", "col"),
        P("row", "col"),
        P(),
        P(),
    )
    out_specs = (P("row", "col"), P("row", "col"), P("col", None))
    return jax.shard_map(
        per_device, mesh=mesh, in_specs=in_specs, out_specs=out_specs, check_vma=False
    )
```

profile of v0, /device:TPU:0, one launch (start us, length us, event | category | flops | bytes accessed | tf_op | source)
XLA Modules:
  0.0 786.2 jit_solution(12624637121962711433)
XLA Ops:
  10.0 52.0 %all-gather.3.cloned.1.call-done = f32[128,4096]{1,0:T(8,128)} async-done(((f32[16,4096]{1,0:T(8,128)}), f32[128,4096]{1,0:T(8,128)}) %all-gather.3.cloned.1.call-update) | async-done | bytes 2097168 | tf_op jit(solution)/shard_map/all_gather | solution.py:153
  74.0 8.1 %reshape.201 = f32[16,16,64,64]{3,2,1,0:T(8,128)} reshape(f32[256,4096]{1,0:T(8,128)} %broadcast_select_fusion.5) | data formatting | bytes 8388608 | tf_op jit(solution)/shard_map/reshape | solution.py:124
  82.1 12.0 %rev.18 = f32[16,16,64,64]{3,2,1,0:T(8,128)} reverse(f32[16,16,64,64]{3,2,1,0:T(8,128)} %reshape.201), dimensions={2} | reverse | bytes 8388608 | tf_op jit(solution)/shard_map/rev | solution.py:116
  94.1 9.8 %broadcast_select_fusion.2 = f32[16,16,64,64]{3,2,1,0:T(8,128)} fusion(f32[16,16,64,64]{3,2,1,0:T(8,128)} %rev.18, f32[16,16,64,64]{3,2,1,0:T(8,128)} %reshape.201, pred[16,16]{1,0:T(8,128)(4,1)S(1)} %get-tuple-element.182), kind=kLoop, calls=%fused_computation.136 | loop fusion | flops 1048576 | bytes 12583168 | tf_op jit(solution)/shard_map/jit(_where)/select_n | solution.py:116
  103.9 13.2 %rev.19 = f32[16,16,64,64]{3,2,1,0:T(8,128)} reverse(f32[16,16,64,64]{3,2,1,0:T(8,128)} %broadcast_select_fusion.2), dimensions={3} | reverse | bytes 8388608 | tf_op jit(solution)/shard_map/rev | solution.py:117
  123.4 9.8 %copy.21 = f32[16,64,16,64]{3,2,1,0:T(8,128)} copy(f32[16,64,16,64]{3,1,2,0:T(8,128)S(1)} %select_bitcast_fusion.1) | data formatting | bytes 8388608 | tf_op jit(solution)/shard_map/transpose | solution.py:126
  133.2 7.6 reshape.202
  171.8 290.4 %while.15 = (s32[]{:T(128)}, f32[4,512,512]{2,1,0:T(8,128)}, f32[4,512,512]{2,1,0:T(8,128)}, f32[8]{0:T(128)S(1)}, f32[2,128,8,128]{3,2,1,0:T(8,128)S(1)}, /*ind...) while((s32[]{:T(128)}, f32[4,512,512]{2,1,0:T(8,128)}, ...), condition=%wide.region_5.7_spmd, body=%wide.region_1.6_spmd.sunk | while | flops 5924732928 | bytes 203478224 | solution.py:172
  481.9 9.2 %copy.45 = f32[16,64,16,64]{3,1,2,0:T(8,128)} copy(f32[16,64,16,64]{3,2,1,0:T(8,128)} %reshape.207) | data formatting | bytes 8388608 | tf_op jit(solution)/shard_map/reshape | solution.py:131
  491.1 11.9 %rev.20 = f32[16,16,64,64]{3,2,1,0:T(8,128)} reverse(f32[16,16,64,64]{3,2,1,0:T(8,128)} %bitcast.205), dimensions={2} | reverse | bytes 8388608 | tf_op jit(solution)/shard_map/rev | solution.py:116
  503.1 11.0 %broadcast_select_fusion.1 = f32[16,16,64,64]{3,2,1,0:T(8,128)} fusion(f32[16,16,64,64]{3,2,1,0:T(8,128)} %rev.20, pred[16,16]{1,0:T(8,128)(4,1)S(1)} %copy-done.8, f32[16,64,16,64]{3,2,1,0:T(8,128)} %reshape.207), kind=kLoop, calls=%fused_computation.135 | loop fusion | flops 1048576 | bytes 12583168 | tf_op jit(solution)/shard_map/jit(_where)/select_n | solution.py:116
  514.0 13.2 %rev.21 = f32[16,16,64,64]{3,2,1,0:T(8,128)} reverse(f32[16,16,64,64]{3,2,1,0:T(8,128)} %broadcast_select_fusion.1), dimensions={3} | reverse | bytes 8388608 | tf_op jit(solution)/shard_map/rev | solution.py:117
  527.2 9.8 %broadcast_select_fusion.3 = f32[16,16,64,64]{3,2,1,0:T(8,128)} fusion(f32[16,16,64,64]{3,2,1,0:T(8,128)} %rev.21, f32[16,16,64,64]{3,2,1,0:T(8,128)} %broadcast_select_fusion.1, pred[16,16]{1,0:T(8,128)(4,1)S(1)} %copy-done.6), kind=kLoop, calls=%fused_computation.137 | loop fusion | flops 1048576 | bytes 12583168 | tf_op jit(solution)/shard_map/jit(_where)/select_n | solution.py:117
  537.1 7.9 %reshape.208 = f32[256,4096]{1,0:T(8,128)} reshape(f32[16,16,64,64]{3,2,1,0:T(8,128)} %broadcast_select_fusion.3) | data formatting | bytes 8388608 | tf_op jit(solution)/shard_map/reshape | solution.py:133
  549.9 67.1 %reduce-scatter.2.cloned.1.call-done = bf16[16,4096]{1,0:T(8,128)(2,1)} async-done(((bf16[128,4096]{1,0:T(8,128)(2,1)}), bf16[16,4096]{1,0:T(8,128)(2,1)}) %reduce-scatter.2.cloned.1.call-update) | async-done | bytes 131088 | tf_op jit(solution)/shard_map/reduce_scatter | solution.py:188
  617.1 33.0 %all-reduce.3.cloned.1.call-done = bf16[16,4096]{1,0:T(8,128)(2,1)} async-done(((bf16[16,4096]{1,0:T(8,128)(2,1)}), bf16[16,4096]{1,0:T(8,128)(2,1)}) %all-reduce.3.cloned.1.call-update) | async-done | bytes 131088 | tf_op jit(solution)/shard_map/psum | solution.py:179
  661.1 32.0 %all-gather.5.cloned.1.call-done = bf16[128,4096]{1,0:T(8,128)(2,1)} async-done(((bf16[16,4096]{1,0:T(8,128)(2,1)}), bf16[128,4096]{1,0:T(8,128)(2,1)}) %all-gather.5.cloned.1.call-update) | async-done | bytes 1048592 | tf_op jit(solution)/shard_map/all_gather | solution.py:191
  704.1 8.1 %reshape.210 = f32[16,16,64,64]{3,2,1,0:T(8,128)} reshape(f32[256,4096]{1,0:T(8,128)} %broadcast_select_fusion.4) | data formatting | bytes 8388608 | tf_op jit(solution)/shard_map/reshape | solution.py:124
  712.2 12.0 %rev.22 = f32[16,16,64,64]{3,2,1,0:T(8,128)} reverse(f32[16,16,64,64]{3,2,1,0:T(8,128)} %reshape.210), dimensions={2} | reverse | bytes 8388608 | tf_op jit(solution)/shard_map/rev | solution.py:116
  724.1 9.8 %broadcast_select_fusion = f32[16,16,64,64]{3,2,1,0:T(8,128)} fusion(f32[16,16,64,64]{3,2,1,0:T(8,128)} %rev.22, f32[16,16,64,64]{3,2,1,0:T(8,128)} %reshape.210, pred[16,16]{1,0:T(8,128)(4,1)S(1)} %copy-done.8), kind=kLoop, calls=%fused_computation.134 | loop fusion | flops 1048576 | bytes 12583168 | tf_op jit(solution)/shard_map/jit(_where)/select_n | solution.py:116
  733.9 13.2 %rev.23 = f32[16,16,64,64]{3,2,1,0:T(8,128)} reverse(f32[16,16,64,64]{3,2,1,0:T(8,128)} %broadcast_select_fusion), dimensions={3} | reverse | bytes 8388608 | tf_op jit(solution)/shard_map/rev | solution.py:117
  753.5 9.8 %copy.25 = f32[16,64,16,64]{3,2,1,0:T(8,128)} copy(f32[16,64,16,64]{3,1,2,0:T(8,128)S(1)} %select_bitcast_fusion) | data formatting | bytes 8388608 | tf_op jit(solution)/shard_map/transpose | solution.py:126
  763.3 7.6 reshape.211
  770.9 8.6 %add_tanh_fusion = f32[1024,1024]{1,0:T(8,128)} fusion(f32[1024,1024]{1,0:T(8,128)} %reshape.211, f32[1024,1024]{1,0:T(8,128)} %param.16, f32[1024,1024]{1,0:T(8,128)} %subtract_multiply_fusion.2), kind=kLoop, calls=%fused_computation.131 | loop fusion | flops 2097152 | bytes 16777216 | tf_op jit(solution)/shard_map/tanh | solution.py:194
  (271 shorter events, 368.1 us)
Async XLA Ops:
  7.2 54.8 %all-gather.3.cloned.1.call-start = ((), (), s32[]{:S(2)}) async-start(), calls=%async_computation.1 | async-start | bytes 2359296 | tf_op jit(solution)/shard_map/all_gather | solution.py:153
  7.9 609.1 %reduce-scatter.2.cloned.1.call-start = ((), (), s32[]{:S(2)}) async-start(), calls=%async_computation.3 | async-start | bytes 1179648 | tf_op jit(solution)/shard_map/reduce_scatter | solution.py:188
  9.2 60.1 %copy-start.11 = (s32[256]{0:T(256)}, s32[256]{0:T(256)S(1)}, u32[]{:S(2)}) copy-start(s32[256]{0:T(256)S(1)} %reshape.200) | copy-start | bytes 3076
  9.2 60.0 %copy-start.10 = (s32[1024]{0:T(1024)}, s32[1024]{0:T(1024)S(1)}, u32[]{:S(2)}) copy-start(s32[1024]{0:T(1024)S(1)} %pad_clamp_fusion) | copy-start | bytes 12292
  9.2 60.0 %copy-start.13 = (pred[256]{0:T(512)(128)(4,1)}, pred[256]{0:T(512)(128)(4,1)S(1)}, u32[]{:S(2)}) copy-start(pred[256]{0:T(512)(128)(4,1)S(1)} %compare_and_fusion) | copy-start | bytes 772
  9.9 84.1 %copy-start.7 = (pred[16,16]{1,0:T(8,128)(4,1)}, pred[16,16]{1,0:T(8,128)(4,1)S(1)}, u32[]{:S(2)}) copy-start(pred[16,16]{1,0:T(8,128)(4,1)S(1)} %get-tuple-element.182) | copy-start | bytes 772
  10.0 107.1 %copy-start.5 = (pred[16,16]{1,0:T(8,128)(4,1)}, pred[16,16]{1,0:T(8,128)(4,1)S(1)}, u32[]{:S(2)}) copy-start(pred[16,16]{1,0:T(8,128)(4,1)S(1)} %get-tuple-element.181) | copy-start | bytes 772
  145.4 4.3 collective-permute-start.1
  146.7 4.0 collective-permute-start
  150.9 20.9 %copy-start.1 = (f32[2,128,8,128]{3,2,1,0:T(8,128)S(1)}, f32[2,128,8,128]{3,2,1,0:T(8,128)}, u32[]{:S(2)}) copy-start(f32[2,128,8,128]{3,2,1,0:T(8,128)} %param.18) | copy-start | bytes 3145732
  150.9 20.8 %copy-start.9 = (f32[8]{0:T(128)S(1)}, f32[8]{0:T(128)}, u32[]{:S(2)}) copy-start(f32[8]{0:T(128)} %param.19) | copy-start | bytes 100
  151.9 9.1 %collective-permute-start.2 = (bf16[1152,64]{1,0:T(8,128)(2,1)}, bf16[1152,64]{1,0:T(8,128)(2,1)}, u32[]{:S(2)}, u32[]{:S(2)}) collective-permute-start(bf16[1152,64]{1,0:T(8,128)(2,1)} %get-tuple-element.178), channel_id=1, source_target_pairs={{0,1},{1,2},{2,3},{3,4},{4,5},{5,6},{6,7},{8,9},{9,10},{10,11},{11... | collective-permute-start | bytes 442376 | tf_op jit(solution)/shard_map/ppermute | solution.py:27
  155.1 11.3 %collective-permute-start.3 = (bf16[1152,64]{1,0:T(8,128)(2,1)}, bf16[1152,64]{1,0:T(8,128)(2,1)}, u32[]{:S(2)}, u32[]{:S(2)}) collective-permute-start(bf16[1152,64]{1,0:T(8,128)(2,1)} %get-tuple-element.177), channel_id=1, source_target_pairs={{1,0},{2,1},{3,2},{4,3},{5,4},{6,5},{7,6},{9,8},{10,9},{11,10},{12... | collective-permute-start | bytes 442376 | tf_op jit(solution)/shard_map/ppermute | solution.py:28
  252.7 4.5 copy-start.2
  320.9 4.5 copy-start.2
  389.1 4.5 copy-start.2
  457.4 4.5 copy-start.2
  467.7 3.5 copy-start.4
  491.1 12.0 %copy-start.8 = (pred[16,16]{1,0:T(8,128)(4,1)S(1)}, pred[16,16]{1,0:T(8,128)(4,1)}, u32[]{:S(2)}) copy-start(pred[16,16]{1,0:T(8,128)(4,1)} %copy-done.7) | copy-start | bytes 772
  514.0 13.2 %copy-start.6 = (pred[16,16]{1,0:T(8,128)(4,1)S(1)}, pred[16,16]{1,0:T(8,128)(4,1)}, u32[]{:S(2)}) copy-start(pred[16,16]{1,0:T(8,128)(4,1)} %copy-done.5) | copy-start | bytes 772
  537.1 7.9 %copy-start.12 = (s32[256]{0:T(256)S(1)}, s32[256]{0:T(256)}, u32[]{:S(2)}) copy-start(s32[256]{0:T(256)} %copy-done.11) | copy-start | bytes 3076
  549.9 100.2 %all-reduce.3.cloned.1.call-start = ((), (), s32[]{:S(2)}) async-start(), calls=%async_computation.4 | async-start | bytes 262144 | tf_op jit(solution)/shard_map/psum | solution.py:179
  617.0 76.1 %all-gather.5.cloned.1.call-start = ((), (), s32[]{:S(2)}) async-start(), calls=%async_computation.2 | async-start | bytes 1179648 | tf_op jit(solution)/shard_map/all_gather | solution.py:191
  694.5 4.8 copy-start.14
  (5 other events, 15.1 us)
Sparse Core Ops, SparseCore 0:
  10.1 51.7 all-gather.2
  550.0 66.9 reduce-scatter.1
  619.3 30.7 all-reduce.2
  652.8 40.2 all-gather.4
where the time goes:
time: 795 us; the launch traced here: 786 us
  matrix products  221 us (28%)
  local copies, waits for them, and re-layouts  208 us (26%)
  waiting for transfers between devices  196 us (25%)
  other arithmetic  111 us (14%)
  loops' own time  27.4 us (3%)
  between operations  14.3 us (2%)
  starting transfers between devices  8.95 us (1%)
    dot_general x48, matrix products, dot_plain(): return jnp.dot(left, right, preferred_element_type=jnp.float32)  105 us
    dot_general x32, matrix products, dot_right_t(): lax.dot_general(left, right, (((1,), (1,)), ((), ())), preferred_element_...  95 us
    reduce_scatter x1, waiting for transfers between devices, per_device(): lax.psum_scatter(whole_sum, 'col', scatter_dimension=0, tiled=True)  67.1 us
    all_gather x1, waiting for transfers between devices, per_device(): everything = lax.all_gather(masters, 'col', axis=0, tiled=True)  52 us
    rev x3, local copies, waits for them, and re-layouts, orient_cells(): cells = jnp.where(flip_second[..., None, None], cells[..., :, ::-1], cells)  39.6 us
    rev x3, local copies, waits for them, and re-layouts, orient_cells(): cells = jnp.where(flip_first[..., None, None], cells[..., ::-1, :], cells)  35.9 us
    psum x1, waiting for transfers between devices, per_device(): lax.psum(jnp.dot(selector, cell_grads, precision=lax.Precision.HIGHEST, p...  33 us
    all_gather x1, waiting for transfers between devices, per_device(): lax.all_gather(fresh.astype(jnp.bfloat16), 'col', axis=0, tiled=True)  32 us
  transfers between devices with their start and end apart: 8, of which 7 were waited for; matrix products, arithmetic and copies ran while one was open for 1% of the time, Pallas kernels for 0%

commit v1 on v0

v1 whole, which is shorter than its diff:
```python
import functools
import math

import jax
import jax.numpy as jnp
import numpy as np
from jax import lax
from jax.experimental import pallas as pl
from jax.experimental.pallas import tpu as pltpu
from jax.sharding import PartitionSpec as P

TILE = 512
TPD = 2
HALO = 64
CELL = 64
LANES = 128
HALF = CELL // 2

step_free = 1.0
step_master = 0.05
resist_gain = 2.0
resist_level = 1.8


def dot(left, right):
    return jnp.dot(left, right, preferred_element_type=jnp.float32)


def tables(pad_side, band_side, halo, tile):
    freqs = np.arange(band_side, dtype=np.int64) - band_side // 2
    phases = (freqs[:, None] * np.arange(pad_side)[None, :]) % pad_side
    angles = phases.astype(np.float32) * np.float32(2.0 * math.pi / pad_side)
    cos = np.cos(angles)
    sin = np.sin(angles)
    cos_in = cos[:, halo : halo + tile]
    sin_in = sin[:, halo : halo + tile]
    cs_full = np.concatenate([cos, sin], 0)
    cs_in = np.concatenate([cos_in, sin_in], 0)
    field = np.block([[cos_in, sin_in], [-sin_in, cos_in]])
    parts = (cs_full, cs_full.T, cs_in, cs_in.T, field, field.T)
    return [jnp.asarray(np.ascontiguousarray(p).astype(jnp.bfloat16)) for p in parts]


def placements():
    rows_place = np.zeros((4, CELL, 2 * CELL), np.float32)
    cols_place = np.zeros((4, LANES, LANES), np.float32)
    for f in range(4):
        for side in range(2):
            flip = (f >> side) & 1
            for r in range(HALF):
                for h in range(2):
                    y = 2 * r + h
                    rows_place[f, CELL - 1 - y if flip else y, side * CELL + h * HALF + r] = 1
            for x in range(CELL):
                cols_place[f, side * CELL + x, side * CELL + (CELL - 1 - x if flip else x)] = 1
    cast = lambda v: jnp.asarray(np.ascontiguousarray(v).astype(jnp.bfloat16))
    return cast(rows_place), cast(rows_place.transpose(0, 2, 1)), cast(cols_place)


def left_mask(rows):
    return lax.broadcasted_iota(jnp.int32, (rows, LANES), 1) < CELL


def pair_codes(inst_ref, orient_ref, owner_ref, a, b):
    s0 = owner_ref[inst_ref[a, b]]
    s1 = owner_ref[inst_ref[a, b + 1]]
    o0 = orient_ref[a, b]
    o1 = orient_ref[a, b + 1]
    return s0, s1, (o0 & 1) + 2 * (o1 & 1), (o0 >> 1) + 2 * (o1 >> 1)


def assemble_pair(table_ref, rows_ref, cols_ref, codes):
    s0, s1, fr, fc = codes
    left = left_mask(HALF)
    p0 = table_ref[s0].astype(jnp.float32)
    p1 = table_ref[s1].astype(jnp.float32)
    q0 = pltpu.roll(p0, CELL, 1)
    q1 = pltpu.roll(p1, CELL, 1)
    parts = [
        jnp.where(left, p0, 0.0),
        jnp.where(left, q0, 0.0),
        jnp.where(left, 0.0, q1),
        jnp.where(left, 0.0, p1),
    ]
    split = jnp.concatenate(parts, axis=0).astype(jnp.bfloat16)
    placed = dot(rows_ref[fr], split).astype(jnp.bfloat16)
    return dot(placed, cols_ref[fc])


def image_kernel(emit_mask, inst_ref, orient_ref, owner_ref, table_ref, free_ref, rows_ref, cols_ref, *outs):
    a = pl.program_id(0)
    for pair in range(free_ref.shape[1] // LANES):
        codes = pair_codes(inst_ref, orient_ref, owner_ref, a, 2 * pair)
        cells = assemble_pair(table_ref, rows_ref, cols_ref, codes)
        lanes = slice(pair * LANES, (pair + 1) * LANES)
        value = jnp.tanh(cells + free_ref[:, lanes])
        outs[0][:, lanes] = value
        if emit_mask:
            outs[1][:, lanes] = value.astype(jnp.bfloat16)


def whole_spec(array):
    zeros = (0,) * array.ndim
    return pl.BlockSpec(array.shape, lambda *_: zeros)


def image(inst, orient, owner, table, free, rows_place, cols_place, emit_mask):
    height, width = free.shape
    strip = pl.BlockSpec((CELL, width), lambda a, *_: (a, 0))
    out_shape = [jax.ShapeDtypeStruct(free.shape, jnp.float32)]
    if emit_mask:
        out_shape.append(jax.ShapeDtypeStruct(free.shape, jnp.bfloat16))
    return pl.pallas_call(
        functools.partial(image_kernel, emit_mask),
        grid_spec=pltpu.PrefetchScalarGridSpec(
            num_scalar_prefetch=3,
            grid=(height // CELL,),
            in_specs=[whole_spec(table), strip, whole_spec(rows_place), whole_spec(cols_place)],
            out_specs=[strip] * len(out_shape),
        ),
        out_shape=out_shape,
        name="image",
    )(inst, orient, owner, table, free, rows_place, cols_place)


def tile_kernel(
    inst_ref, orient_ref, owner_ref, weights_ref,
    padded_ref, target_ref, shading_ref, free_ref, spectra_ref,
    cs_full_ref, cs_full_t_ref, cs_in_ref, cs_in_t_ref, field_ref, field_t_ref,
    rows_t_ref, cols_ref,
    resist_ref, new_free_ref, sums_ref,
    amp_s, half_s, bhalf_s, field_s, grad_s, sums_s,
):
    i = pl.program_id(0)
    j = pl.program_id(1)
    band = spectra_ref.shape[1]
    kernels = spectra_ref.shape[2]
    tile = target_ref.shape[0]
    pad_side = cs_full_ref.shape[1]
    block = field_s.shape[1]
    wide = 2 * band

    @pl.when((i == 0) & (j == 0))
    def _():
        sums_s[...] = jnp.zeros_like(sums_s)

    window = padded_ref[
        pl.ds(pl.multiple_of(i * tile, 128), pad_side), pl.ds(pl.multiple_of(j * tile, 128), pad_side)
    ]
    forw = dot(cs_full_ref[...], window).astype(jnp.bfloat16)
    spec = dot(forw, cs_full_t_ref[...])
    spec_re = (spec[:band, :band] + spec[band:, band:]) / pad_side
    spec_im = (spec[band:, :band] - spec[:band, band:]) / pad_side
    for k in range(kernels):
        kern_re = spectra_ref[0, :, k, :]
        kern_im = spectra_ref[1, :, k, :]
        amp_re = (kern_re * spec_re - kern_im * spec_im).astype(jnp.bfloat16)
        amp_im = (kern_re * spec_im + kern_im * spec_re).astype(jnp.bfloat16)
        at = k * wide
        amp_s[:band, at : at + band] = amp_re
        amp_s[band:, at : at + band] = -amp_im
        amp_s[:band, at + band : at + wide] = amp_im
        amp_s[band:, at + band : at + wide] = amp_re
    for k in range(kernels):
        cols = slice(k * wide, (k + 1) * wide)
        half_s[:, cols] = dot(cs_in_t_ref[...], amp_s[:, cols]).astype(jnp.bfloat16)

    def rows_step(n, carry):
        rows = pl.ds(pl.multiple_of(n * block, block), block)
        intensity = jnp.zeros((block, tile), jnp.float32)
        for k in range(kernels):
            field = dot(half_s[rows, k * wide : (k + 1) * wide], field_ref[...])
            field_s[k] = field
            re = field[:, :tile]
            im = field[:, tile:]
            intensity += (weights_ref[k] / (band * band)) * (re * re + im * im)
        resist = jax.nn.sigmoid(resist_gain * (intensity - resist_level))
        resist_ref[rows, :] = resist
        slopes = 2.0 * (resist - target_ref[rows, :]) * resist_gain * resist * (1.0 - resist)
        for k in range(kernels):
            scale = slopes * (2.0 * weights_ref[k] / (band * band))
            re = (field_s[k, :, :tile] * scale).astype(jnp.bfloat16)
            im = (field_s[k, :, tile:] * scale).astype(jnp.bfloat16)
            back = jnp.concatenate([re, im], axis=1)
            bhalf_s[rows, k * wide : (k + 1) * wide] = dot(back, field_t_ref[...]).astype(jnp.bfloat16)
        return carry

    lax.fori_loop(0, tile // block, rows_step, 0)
    bspec_re = jnp.zeros((band, band), jnp.float32)
    bspec_im = jnp.zeros((band, band), jnp.float32)
    for k in range(kernels):
        bamp = dot(cs_in_ref[...], bhalf_s[:, k * wide : (k + 1) * wide])
        bamp_re = bamp[:band, :band] + bamp[band:, band:]
        bamp_im = bamp[:band, band:] - bamp[band:, :band]
        kern_re = spectra_ref[0, :, k, :]
        kern_im = spectra_ref[1, :, k, :]
        bspec_re += kern_re * bamp_re + kern_im * bamp_im
        bspec_im += kern_re * bamp_im - kern_im * bamp_re
    bspec = jnp.concatenate([bspec_re / pad_side, bspec_im / pad_side], axis=1).astype(jnp.bfloat16)
    bforw = dot(bspec, field_ref[...]).astype(jnp.bfloat16)
    bforw = jnp.concatenate([bforw[:, :tile], bforw[:, tile:]], axis=0)
    gradient = dot(cs_in_t_ref[...], bforw)
    shading = shading_ref[...]
    grad_param = gradient * (1.0 - shading * shading)
    new_free_ref[...] = free_ref[...] - step_free * grad_param
    grad_s[...] = grad_param.astype(jnp.bfloat16)
    cells = tile // CELL
    left = left_mask(HALF)

    def cells_step(a, carry):
        rows = pl.ds(pl.multiple_of(a * CELL, CELL), CELL)
        for pair in range(cells // 2):
            s0, s1, fr, fc = pair_codes(
                inst_ref, orient_ref, owner_ref, i * cells + a, j * cells + 2 * pair
            )
            piece = grad_s[rows, pair * LANES : (pair + 1) * LANES]
            turned = dot(piece, cols_ref[fc]).astype(jnp.bfloat16)
            split = dot(rows_t_ref[fr], turned)
            a0 = split[:HALF]
            a1 = pltpu.roll(split[HALF : 2 * HALF], CELL, 1)
            b0 = pltpu.roll(split[2 * HALF : 3 * HALF], CELL, 1)
            b1 = split[3 * HALF :]
            sums_s[s0] += jnp.where(left, a0, a1)
            sums_s[s1] += jnp.where(left, b0, b1)
        return carry

    lax.fori_loop(0, cells, cells_step, 0)

    @pl.when((i == pl.num_programs(0) - 1) & (j == pl.num_programs(1) - 1))
    def _():
        sums_ref[...] = sums_s[...].astype(jnp.bfloat16)


def tile_steps(inst, orient, owner, weights, padded, target, shading, free, spectra, consts, rows_t, cols_place, masters):
    height, width = target.shape
    band = spectra.shape[1]
    kernels = spectra.shape[2]
    block = 64
    tile_spec = pl.BlockSpec((TILE, TILE), lambda i, j, *_: (i, j))
    sums_shape = (masters, HALF, LANES)
    once = [padded, None, None, None, spectra, *consts, rows_t, cols_place]
    return pl.pallas_call(
        tile_kernel,
        grid_spec=pltpu.PrefetchScalarGridSpec(
            num_scalar_prefetch=4,
            grid=(height // TILE, width // TILE),
            in_specs=[tile_spec if v is None else whole_spec(v) for v in once],
            out_specs=[tile_spec, tile_spec, pl.BlockSpec(sums_shape, lambda *_: (0, 0, 0))],
            scratch_shapes=[
                pltpu.VMEM((2 * band, kernels * 2 * band), jnp.bfloat16),
                pltpu.VMEM((TILE, kernels * 2 * band), jnp.bfloat16),
                pltpu.VMEM((TILE, kernels * 2 * band), jnp.bfloat16),
                pltpu.VMEM((kernels, block, 2 * TILE), jnp.float32),
                pltpu.VMEM((TILE, TILE), jnp.bfloat16),
                pltpu.VMEM(sums_shape, jnp.float32),
            ],
        ),
        out_shape=[
            jax.ShapeDtypeStruct(target.shape, jnp.float32),
            jax.ShapeDtypeStruct(target.shape, jnp.float32),
            jax.ShapeDtypeStruct(sums_shape, jnp.bfloat16),
        ],
        compiler_params=pltpu.CompilerParams(vmem_limit_bytes=60 * 1024 * 1024),
        name="tile_steps",
    )(inst, orient, owner, weights, padded, target, shading, free, spectra, *consts, rows_t, cols_place)


def smooth_packed(cells):
    lane = lax.broadcasted_iota(jnp.int32, cells.shape, cells.ndim - 1)
    x = lane % CELL
    before = jnp.where(x == 0, 0.0, jnp.roll(cells, 1, axis=-1))
    after = jnp.where(x == CELL - 1, 0.0, jnp.roll(cells, -1, axis=-1))
    other = jnp.roll(cells, CELL, axis=-1)
    edge = jnp.zeros_like(other[:, :1])
    up = jnp.concatenate([edge, other[:, :-1]], axis=1)
    down = jnp.concatenate([other[:, 1:], edge], axis=1)
    beside = before + after + other + jnp.where(lane < CELL, up, down)
    return 0.5 * cells + 0.125 * beside


def padded_2(value, sides, width):
    for axis, dim in sides:
        peers, length = (lax.axis_size(axis), value.shape[dim])
        up = [(i, (i + 1) % peers) for i in range(peers - 1)]
        down = [(j, i) for i, j in up]
        last = lax.slice_in_dim(value, length - width, length, axis=dim)
        initial = lax.slice_in_dim(value, 0, width, axis=dim)
        before = lax.ppermute(last, axis, up)
        after = lax.ppermute(initial, axis, down)
        value = jnp.concatenate([before, value, after], axis=dim)
    return value


def per_device(
    masters, inst_master, inst_orient, owner_map, tile_free, target, kernel_spectra, socs_weights
):
    stored = masters.shape[0]
    total = owner_map.shape[0]
    consts = tables(TILE + 2 * HALO, kernel_spectra.shape[1], HALO, TILE)
    rows_place, rows_t, cols_place = placements()
    own = masters.reshape(stored, HALF, LANES)
    table = lax.all_gather(own.astype(jnp.bfloat16), "col", axis=0, tiled=True)
    shading, mask = image(
        inst_master, inst_orient, owner_map, table, tile_free, rows_place, cols_place, True
    )
    padded = padded_2(mask, (("row", 0), ("col", 1)), HALO)
    resist, new_free, sums = tile_steps(
        inst_master, inst_orient, owner_map, socs_weights, padded, target, shading, tile_free,
        kernel_spectra, consts, rows_t, cols_place, total,
    )
    part = lax.psum_scatter(sums, "col", scatter_dimension=0, tiled=True)
    summed = lax.psum(part, "row").astype(jnp.float32)
    fresh = smooth_packed(own - step_master * summed).astype(jnp.bfloat16)
    table = lax.all_gather(fresh, "col", axis=0, tiled=True)
    (new_mask,) = image(
        inst_master, inst_orient, owner_map, table, new_free, rows_place, cols_place, False
    )
    return (resist, new_mask, fresh.astype(jnp.float32).reshape(masters.shape))


def solution(mesh):
    in_specs = (
        P("col", None),
        P("row", "col"),
        P("row", "col"),
        P(),
        P("row", "col"),
        P("row", "col"),
        P(),
        P(),
    )
    out_specs = (P("row", "col"), P("row", "col"), P("col", None))
    return jax.shard_map(
        per_device, mesh=mesh, in_specs=in_specs, out_specs=out_specs, check_vma=False
    )
```

time: 795 us -> 364 us (0.46)
  matrix products: 221 us -> 0 us
  local copies, waits for them, and re-layouts: 208 us -> 10 us
  Pallas kernels: 0 us -> 134 us
  other arithmetic: 111 us -> 2.78 us
  loops' own time: 27.4 us -> 0 us
    dot_general x105 -> x0, matrix products: 221 us -> none  [the longest x48 105 us: dot_plain(): return jnp.dot(left, right, preferred_element_type=jnp.float32)]
    pallas_call x0 -> x3, Pallas kernels: none -> 134 us  [the longest x1 104 us: tile_steps(): pl.pallas_call(tile_kernel, grid_spec=pltpu.PrefetchScalarGridSpec(num_sc...]
    rev x6 -> x0, local copies, waits for them, and re-layouts: 75.5 us -> none  [the longest x3 39.6 us: orient_cells(): cells = jnp.where(flip_second[..., None, None], cells[..., :, ::-1], cells)]
    reshape x27 -> x0, local copies, waits for them, and re-layouts: 74.8 us -> none  [the longest x2 16.5 us: cells_of(): image.reshape(grid_rows, cell_side, grid_cols, cell_side)]
    select_n x7 -> x0, other arithmetic: 50 us -> none  [the longest x3 30.5 us: orient_cells(): cells = jnp.where(flip_first[..., None, None], cells[..., ::-1, :], cells)]
    another operation x1 -> x0, loops' own time: 27.4 us -> none  [per_device(): lax.map(one_tile, jnp.arange(TPD * TPD, dtype=jnp.int32))]
    transpose x2 -> x0, local copies, waits for them, and re-layouts: 19.6 us -> none  [assemble(): cells.transpose(0, 2, 1, 3)]
    convert_element_type x11 -> x2, other arithmetic: 14.6 us -> 1.61 us  [the longest x1 0.94 us: per_device(): fresh = smooth_packed(own - step_master * summed).astype(jnp.bfloat16)]
where the time goes in v1:
time: 364 us; the launch traced here: 363 us
  waiting for transfers between devices  196 us (54%)
  Pallas kernels  134 us (37%)
  between operations  13.9 us (4%)
  local copies, waits for them, and re-layouts  10 us (3%)
  starting transfers between devices  6.51 us (2%)
    pallas_call x1, Pallas kernels, tile_steps(): pl.pallas_call(tile_kernel, grid_spec=pltpu.PrefetchScalarGridSpec(num_sc...  104 us
    reduce_scatter x1, waiting for transfers between devices, per_device(): part = lax.psum_scatter(sums, 'col', scatter_dimension=0, tiled=True)  69 us
    all_gather x1, waiting for transfers between devices, per_device(): table = lax.all_gather(own.astype(jnp.bfloat16), 'col', axis=0, tiled=True)  44.7 us
    all_gather x1, waiting for transfers between devices, per_device(): table = lax.all_gather(fresh, 'col', axis=0, tiled=True)  38.8 us
    psum x1, waiting for transfers between devices, per_device(): summed = lax.psum(part, 'row').astype(jnp.float32)  33 us
    pallas_call x2, Pallas kernels, image(): pl.pallas_call(functools.partial(image_kernel, emit_mask), grid_spec=pltp...  29.9 us
  transfers between devices with their start and end apart: 8, of which 7 were waited for; matrix products, arithmetic and copies ran while one was open for 1% of the time, Pallas kernels for 0%

profile of v1, /device:TPU:0, one launch (start us, length us, event | category | flops | bytes accessed | tf_op | source)
XLA Modules:
  0.0 363.0 jit_solution(13262963959526090614)
XLA Ops:
  7.2 1.0 copy.20
  8.2 0.7 bitcast_convert_fusion
  9.0 44.7 %all-gather.3.cloned.1.call-done.table_ref = bf16[128,32,128]{2,1,0:T(8,128)(2,1)} async-done(((bf16[16,32,128]{2,1,0:T(8,128)(2,1)}), bf16[128,32,128]{2,1,0:T(8,128)(2,1)}) %all-gather.3.cloned.1.call-update) | async-done | bytes 1048592 | tf_op jit(solution)/shard_map/all_gather | solution.py:302
  53.7 15.1 %image.2 = (f32[1024,1024]{1,0:T(8,128)}, bf16[1024,1024]{1,0:T(8,128)(2,1)}) custom-call(s32[16,16]{1,0:T(8,128)} %inst_ref.5, s32[16,16]{1,0:T(8,128)} %orient_ref.5, s32[128]{0:T(128)} %owner_ref.5, bf16[128,32,128]{2,1,0:T(8,128)(2,1)} %all-gather.3.cloned.1.call-done.table_ref, f32[1024,1024]{1,0:T(8,128)} %free_ref.3, ...), custom_call_target="tpu_custom_call" | custom-call | tf_op jit(solution)/shard_map/image/pallas_call | solution.py:113
  68.9 1.0 fusion.7
  69.8 1.3 collective-permute-start
  71.1 1.3 collective-permute-start.1
  72.5 1.8 constant_dynamic-update-slice_fusion.1
  74.2 1.8 collective-permute-done.1
  76.1 0.2 fusion.6
  76.3 2.5 collective-permute-start.2
  78.8 1.3 collective-permute-start.3
  80.1 3.5 collective-permute-done.2
  83.6 4.7 %collective-permute-done.3 = bf16[1152,64]{1,0:T(8,128)(2,1)S(1)} collective-permute-done((bf16[1152,64]{1,0:T(8,128)(2,1)S(1)}, bf16[1152,64]{1,0:T(8,128)(2,1)S(1)}, u32[]{:S(2)}, u32[]{:S(2)}) %collective-permute-start.3) | collective-permute-done | bytes 147488 | tf_op jit(solution)/shard_map/ppermute | solution.py:289
  88.3 4.0 %concatenate.25.padded_ref = bf16[1152,1152]{1,0:T(8,128)(2,1)} concatenate(bf16[1152,64]{1,0:T(8,128)(2,1)S(1)} %collective-permute-done.2, bf16[1152,1024]{1,0:T(8,128)(2,1)S(1)} %constant_dynamic-update-slice_fusion, bf16[1152,64]{1,0:T(8,128)(2,1)S(1)} %collective-permute-done.3), dimensions={1} | concatenate | bytes 5308416 | tf_op jit(solution)/shard_map/concatenate | solution.py:290
  92.3 104.4 %tile_steps.1 = (f32[1024,1024]{1,0:T(8,128)}, f32[1024,1024]{1,0:T(8,128)}, bf16[128,32,128]{2,1,0:T(8,128)(2,1)}) custom-call(s32[16,16]{1,0:T(8,128)} %inst_ref.5, s32[16,16]{1,0:T(8,128)} %orient_ref.5, s32[128]{0:T(128)} %owner_ref.5, f32[8]{0:T(128)} %weights_ref.1, bf16[1152,1152]{1,0:T(8,128)(2,1)} %concatenate.25.padded_ref, ...), custom_call_target="tpu_custom_call" | custom-call | tf_op jit(solution)/shard_map/tile_steps/pallas_call | solution.py:242
  196.7 69.0 %reduce-scatter.2.cloned.1.call-done = bf16[16,32,128]{2,1,0:T(8,128)(2,1)} async-done(((bf16[128,32,128]{2,1,0:T(8,128)(2,1)}), bf16[16,32,128]{2,1,0:T(8,128)(2,1)}) %reduce-scatter.2.cloned.1.call-update) | async-done | bytes 131088 | tf_op jit(solution)/shard_map/reduce_scatter | solution.py:311
  265.8 33.0 %all-reduce.4.cloned.1.call-done = bf16[16,32,128]{2,1,0:T(8,128)(2,1)} async-done(((bf16[16,32,128]{2,1,0:T(8,128)(2,1)}), bf16[16,32,128]{2,1,0:T(8,128)(2,1)}) %all-reduce.4.cloned.1.call-update) | async-done | bytes 131088 | tf_op jit(solution)/shard_map/psum | solution.py:312
  298.8 0.9 bitcast_subtract_fusion
  300.1 0.2 slice_maximum_fusion.1
  300.3 0.9 fusion.5
  301.3 1.7 copy.23
  303.0 38.8 %all-gather.5.cloned.1.call-done.table_ref = bf16[128,32,128]{2,1,0:T(8,128)(2,1)} async-done(((bf16[16,32,128]{2,1,0:T(8,128)(2,1)}), bf16[128,32,128]{2,1,0:T(8,128)(2,1)}) %all-gather.5.cloned.1.call-update) | async-done | bytes 1048592 | tf_op jit(solution)/shard_map/all_gather | solution.py:314
  341.7 14.8 %image.3 = f32[1024,1024]{1,0:T(8,128)} custom-call(s32[16,16]{1,0:T(8,128)} %inst_ref.5, s32[16,16]{1,0:T(8,128)} %orient_ref.5, s32[128]{0:T(128)} %owner_ref.5, bf16[128,32,128]{2,1,0:T(8,128)(2,1)} %all-gather.5.cloned.1.call-done.table_ref, f32[1024,1024]{1,0:T(8,128)} %get-tuple-element.12.free_ref, bf16[4,64,128]{2,1,0:T(8,128)(2,1)} %constant.52.clone.rows_ref, ...), custom_call_target="tpu_custom_call" | custom-call | tf_op jit(solution)/shard_map/image/pallas_call | solution.py:113
  (16 shorter events, 0.7 us)
Async XLA Ops:
  7.2 46.5 %all-gather.3.cloned.1.call-start = ((), (), s32[]{:S(2)}) async-start(), calls=%async_computation.1 | async-start | bytes 1179648 | tf_op jit(solution)/shard_map/all_gather | solution.py:302
  8.9 256.8 %reduce-scatter.2.cloned.1.call-start = ((), (), s32[]{:S(2)}) async-start(), calls=%async_computation.2 | async-start | bytes 1179648 | tf_op jit(solution)/shard_map/reduce_scatter | solution.py:311
  69.8 2.6 collective-permute-start
  71.1 4.9 %collective-permute-start.1 = (bf16[64,1024]{1,0:T(8,128)(2,1)S(1)}, bf16[64,1024]{1,0:T(8,128)(2,1)S(1)}, u32[]{:S(2)}, u32[]{:S(2)}) collective-permute-start(bf16[64,1024]{1,0:T(8,128)(2,1)S(1)} %get-tuple-element.15), channel_id=1, source_target_pairs={{8,0},{16,8},{24,16},{9,1},{17,9},{25,17},{10,2},{18,10},{26,18},{... | collective-permute-start | bytes 393224 | tf_op jit(solution)/shard_map/ppermute | solution.py:289
  76.3 7.3 %collective-permute-start.2 = (bf16[1152,64]{1,0:T(8,128)(2,1)S(1)}, bf16[1152,64]{1,0:T(8,128)(2,1)S(1)}, u32[]{:S(2)}, u32[]{:S(2)}) collective-permute-start(bf16[1152,64]{1,0:T(8,128)(2,1)S(1)} %get-tuple-element.14), channel_id=1, source_target_pairs={{0,1},{1,2},{2,3},{3,4},{4,5},{5,6},{6,7},{8,9},{9,10},{10,11},{11... | collective-permute-start | bytes 442376 | tf_op jit(solution)/shard_map/ppermute | solution.py:288
  78.8 9.5 %collective-permute-start.3 = (bf16[1152,64]{1,0:T(8,128)(2,1)S(1)}, bf16[1152,64]{1,0:T(8,128)(2,1)S(1)}, u32[]{:S(2)}, u32[]{:S(2)}) collective-permute-start(bf16[1152,64]{1,0:T(8,128)(2,1)S(1)} %get-tuple-element.13), channel_id=1, source_target_pairs={{1,0},{2,1},{3,2},{4,3},{5,4},{6,5},{7,6},{9,8},{10,9},{11,10},{12... | collective-permute-start | bytes 442376 | tf_op jit(solution)/shard_map/ppermute | solution.py:289
  196.7 102.1 %all-reduce.4.cloned.1.call-start = ((), (), s32[]{:S(2)}) async-start(), calls=%async_computation.3 | async-start | bytes 262144 | tf_op jit(solution)/shard_map/psum | solution.py:312
  265.7 76.0 %all-gather.5.cloned.1.call-start = ((), (), s32[]{:S(2)}) async-start(), calls=%async_computation.4 | async-start | bytes 1179648 | tf_op jit(solution)/shard_map/all_gather | solution.py:314
Sparse Core Ops, SparseCore 0:
  10.7 42.9 all-gather.2
  196.8 68.8 reduce-scatter.1
  268.0 30.6 all-reduce.3
  301.4 40.2 all-gather.4

commit v2 on v1

--- a/solution.py
+++ b/solution.py
@@ -15,6 +15,7 @@
 CELL = 64
 LANES = 128
 HALF = CELL // 2
+BLOCK = 256
 
 step_free = 1.0
 step_master = 0.05
@@ -35,9 +36,10 @@
     cos_in = cos[:, halo : halo + tile]
     sin_in = sin[:, halo : halo + tile]
     cs_full = np.concatenate([cos, sin], 0)
+    cs_lanes = np.pad(cs_full, ((0, 0), (LANES - halo, LANES - halo)))
     cs_in = np.concatenate([cos_in, sin_in], 0)
     field = np.block([[cos_in, sin_in], [-sin_in, cos_in]])
-    parts = (cs_full, cs_full.T, cs_in, cs_in.T, field, field.T)
+    parts = (cs_full, cs_lanes.T, cs_in, cs_in.T, field, field.T)
     return [jnp.asarray(np.ascontiguousarray(p).astype(jnp.bfloat16)) for p in parts]
 
 
@@ -137,6 +139,7 @@
     kernels = spectra_ref.shape[2]
     tile = target_ref.shape[0]
     pad_side = cs_full_ref.shape[1]
+    pad_lanes = cs_full_t_ref.shape[0]
     block = field_s.shape[1]
     wide = 2 * band
 
@@ -145,7 +148,7 @@
         sums_s[...] = jnp.zeros_like(sums_s)
 
     window = padded_ref[
-        pl.ds(pl.multiple_of(i * tile, 128), pad_side), pl.ds(pl.multiple_of(j * tile, 128), pad_side)
+        pl.ds(pl.multiple_of(i * tile, 128), pad_side), pl.ds(pl.multiple_of(j * tile, 128), pad_lanes)
     ]
     forw = dot(cs_full_ref[...], window).astype(jnp.bfloat16)
     spec = dot(forw, cs_full_t_ref[...])
@@ -235,7 +238,7 @@
     height, width = target.shape
     band = spectra.shape[1]
     kernels = spectra.shape[2]
-    block = 64
+    block = BLOCK
     tile_spec = pl.BlockSpec((TILE, TILE), lambda i, j, *_: (i, j))
     sums_shape = (masters, HALF, LANES)
     once = [padded, None, None, None, spectra, *consts, rows_t, cols_place]
@@ -265,30 +268,237 @@
     )(inst, orient, owner, weights, padded, target, shading, free, spectra, *consts, rows_t, cols_place)
 
 
+MESH = pl.DeviceIdType.MESH
+VM = pl.BlockSpec(memory_space=pltpu.VMEM)
+
+
+def split_id(flat, n_col):
+    return (lax.div(flat, n_col), lax.rem(flat, n_col))
+
+
+def greet(peers):
+    barrier = pltpu.get_barrier_semaphore()
+    for peer in peers:
+        pl.semaphore_signal(barrier, inc=1, device_id=peer, device_id_type=MESH)
+    pl.semaphore_wait(barrier, len(peers))
+
+
+def gather_kernel(n_col, own_ref, table_ref, send_sem, recv_sem):
+    r = lax.axis_index("row")
+    c = lax.axis_index("col")
+    stored = own_ref.shape[0]
+    greet([(r, lax.rem(c + t, n_col)) for t in range(1, n_col)])
+    here = table_ref.at[pl.ds(c * stored, stored)]
+    copies = [
+        pltpu.make_async_remote_copy(
+            src_ref=own_ref,
+            dst_ref=here,
+            send_sem=send_sem.at[t],
+            recv_sem=recv_sem.at[t],
+            device_id=(r, lax.rem(c + t, n_col)),
+            device_id_type=MESH,
+        )
+        for t in range(1, n_col)
+    ]
+    for copy in copies:
+        copy.start()
+    table_ref[pl.ds(c * stored, stored)] = own_ref[...]
+    for copy in copies:
+        copy.wait()
+
+
+def gather_masters(own, n_col):
+    return pl.pallas_call(
+        functools.partial(gather_kernel, n_col),
+        in_specs=[VM],
+        out_specs=VM,
+        out_shape=jax.ShapeDtypeStruct((n_col * own.shape[0],) + own.shape[1:], own.dtype),
+        scratch_shapes=[pltpu.SemaphoreType.DMA((n_col,)), pltpu.SemaphoreType.DMA((n_col,))],
+        compiler_params=pltpu.CompilerParams(collective_id=0, has_side_effects=True),
+        name="gather_masters",
+    )(own)
+
+
+def halo_kernel(n_row, n_col, mask_ref, out_ref, send_sem, recv_sem):
+    r = lax.axis_index("row")
+    c = lax.axis_index("col")
+    height, width = mask_ref.shape
+    row_parts = {
+        -1: (slice(0, HALO), slice(HALO + height, 2 * HALO + height)),
+        0: (slice(0, height), slice(HALO, HALO + height)),
+        1: (slice(height - HALO, height), slice(0, HALO)),
+    }
+    col_parts = {
+        -1: (slice(0, LANES), slice(LANES + width, 2 * LANES + width)),
+        0: (slice(0, width), slice(LANES, LANES + width)),
+        1: (slice(width - LANES, width), slice(0, LANES)),
+    }
+    moves = [(0, 1), (0, -1), (1, 0), (-1, 0), (1, 1), (1, -1), (-1, 1), (-1, -1)]
+    ids = [(lax.rem(r + n_row + dr, n_row), lax.rem(c + n_col + dc, n_col)) for dr, dc in moves]
+    greet(ids)
+    copies = []
+    for at, (dr, dc) in enumerate(moves):
+        src_rows, dst_rows = row_parts[dr]
+        src_cols, dst_cols = col_parts[dc]
+        copy = pltpu.make_async_remote_copy(
+            src_ref=mask_ref.at[src_rows, src_cols],
+            dst_ref=out_ref.at[dst_rows, dst_cols],
+            send_sem=send_sem.at[at],
+            recv_sem=recv_sem.at[at],
+            device_id=ids[at],
+            device_id_type=MESH,
+        )
+        copy.start()
+        copies.append(copy)
+    out_ref[HALO : HALO + height, LANES : LANES + width] = mask_ref[...]
+    for copy in copies:
+        copy.wait()
+
+    @pl.when(r == 0)
+    def _():
+        out_ref[:HALO, :] = jnp.zeros((HALO, width + 2 * LANES), out_ref.dtype)
+
+    @pl.when(r == n_row - 1)
+    def _():
+        out_ref[HALO + height :, :] = jnp.zeros((HALO, width + 2 * LANES), out_ref.dtype)
+
+    @pl.when(c == 0)
+    def _():
+        out_ref[:, :LANES] = jnp.zeros((height + 2 * HALO, LANES), out_ref.dtype)
+
+    @pl.when(c == n_col - 1)
+    def _():
+        out_ref[:, LANES + width :] = jnp.zeros((height + 2 * HALO, LANES), out_ref.dtype)
+
+
+def with_halo(mask, n_row, n_col):
+    height, width = mask.shape
+    return pl.pallas_call(
+        functools.partial(halo_kernel, n_row, n_col),
+        in_specs=[VM],
+        out_specs=VM,
+        out_shape=jax.ShapeDtypeStruct((height + 2 * HALO, width + 2 * LANES), mask.dtype),
+        scratch_shapes=[pltpu.SemaphoreType.DMA((8,)), pltpu.SemaphoreType.DMA((8,))],
+        compiler_params=pltpu.CompilerParams(collective_id=1, has_side_effects=True),
+        name="with_halo",
+    )(mask)
+
+
 def smooth_packed(cells):
-    lane = lax.broadcasted_iota(jnp.int32, cells.shape, cells.ndim - 1)
+    count = cells.shape[0]
+    flat = cells.reshape(count * HALF, LANES)
+    lane = lax.broadcasted_iota(jnp.int32, flat.shape, 1)
     x = lane % CELL
-    before = jnp.where(x == 0, 0.0, jnp.roll(cells, 1, axis=-1))
-    after = jnp.where(x == CELL - 1, 0.0, jnp.roll(cells, -1, axis=-1))
-    other = jnp.roll(cells, CELL, axis=-1)
-    edge = jnp.zeros_like(other[:, :1])
-    up = jnp.concatenate([edge, other[:, :-1]], axis=1)
-    down = jnp.concatenate([other[:, 1:], edge], axis=1)
+    row = lax.broadcasted_iota(jnp.int32, flat.shape, 0) % HALF
+    before = jnp.where(x == 0, 0.0, pltpu.roll(flat, 1, 1))
+    after = jnp.where(x == CELL - 1, 0.0, pltpu.roll(flat, LANES - 1, 1))
+    other = pltpu.roll(flat, CELL, 1)
+    up = jnp.where(row == 0, 0.0, pltpu.roll(other, 1, 0))
+    down = jnp.where(row == HALF - 1, 0.0, pltpu.roll(other, count * HALF - 1, 0))
     beside = before + after + other + jnp.where(lane < CELL, up, down)
-    return 0.5 * cells + 0.125 * beside
-
-
-def padded_2(value, sides, width):
-    for axis, dim in sides:
-        peers, length = (lax.axis_size(axis), value.shape[dim])
-        up = [(i, (i + 1) % peers) for i in range(peers - 1)]
-        down = [(j, i) for i, j in up]
-        last = lax.slice_in_dim(value, length - width, length, axis=dim)
-        initial = lax.slice_in_dim(value, 0, width, axis=dim)
-        before = lax.ppermute(last, axis, up)
-        after = lax.ppermute(initial, axis, down)
-        value = jnp.concatenate([before, value, after], axis=dim)
-    return value
+    return (0.5 * flat + 0.125 * beside).reshape(cells.shape)
+
+
+def update_kernel(
+    n_row, n_col, sums_ref, own_ref, table_ref,
+    parts, fresh, send_sem, recv_sem, send2_sem, recv2_sem,
+):
+    r = lax.axis_index("row")
+    c = lax.axis_index("col")
+    count = n_row * n_col
+    me = r * n_col + c
+    stored = own_ref.shape[0]
+    share = stored // n_row
+    barrier = pltpu.get_barrier_semaphore()
+
+    def first_row(flat):
+        pr, pc = split_id(flat, n_col)
+        return pc * stored + pr * share
+
+    def hello(t, carry):
+        pl.semaphore_signal(
+            barrier, inc=1, device_id=split_id(lax.rem(me + t, count), n_col), device_id_type=MESH
+        )
+        return carry
+
+    lax.fori_loop(1, count, hello, 0)
+    pl.semaphore_wait(barrier, count - 1)
+
+    def part_copy(t):
+        peer = lax.rem(me + t, count)
+        return pltpu.make_async_remote_copy(
+            src_ref=sums_ref.at[pl.ds(first_row(peer), share)],
+            dst_ref=parts.at[t],
+            send_sem=send_sem.at[t],
+            recv_sem=recv_sem.at[t],
+            device_id=split_id(peer, n_col),
+            device_id_type=MESH,
+        )
+
+    def start_part(t, carry):
+        part_copy(t).start()
+        return carry
+
+    lax.fori_loop(1, count, start_part, 0)
+
+    def add_part(t, total):
+        part_copy(t).wait_recv()
+        return total + parts[t].astype(jnp.float32)
+
+    mine = first_row(me)
+    total = lax.fori_loop(1, count, add_part, sums_ref[pl.ds(mine, share)].astype(jnp.float32))
+    updated = own_ref[pl.ds(r * share, share)] - step_master * total
+    value = smooth_packed(updated).astype(jnp.bfloat16)
+    fresh[...] = value
+    table_ref[pl.ds(mine, share)] = value
+
+    def end_part(t, carry):
+        part_copy(t).wait_send()
+        return carry
+
+    lax.fori_loop(1, count, end_part, 0)
+
+    def fresh_copy(t):
+        return pltpu.make_async_remote_copy(
+            src_ref=fresh,
+            dst_ref=table_ref.at[pl.ds(mine, share)],
+            send_sem=send2_sem.at[t],
+            recv_sem=recv2_sem.at[t],
+            device_id=split_id(lax.rem(me + t, count), n_col),
+            device_id_type=MESH,
+        )
+
+    def start_fresh(t, carry):
+        fresh_copy(t).start()
+        return carry
+
+    def end_fresh(t, carry):
+        fresh_copy(t).wait()
+        return carry
+
+    lax.fori_loop(1, count, start_fresh, 0)
+    lax.fori_loop(1, count, end_fresh, 0)
+
+
+def update_masters(sums, own, n_row, n_col):
+    count = n_row * n_col
+    piece = (own.shape[0] // n_row,) + own.shape[1:]
+    return pl.pallas_call(
+        functools.partial(update_kernel, n_row, n_col),
+        in_specs=[VM, VM],
+        out_specs=VM,
+        out_shape=jax.ShapeDtypeStruct(sums.shape, jnp.bfloat16),
+        scratch_shapes=[
+            pltpu.VMEM((count,) + piece, jnp.bfloat16),
+            pltpu.VMEM(piece, jnp.bfloat16),
+            pltpu.SemaphoreType.DMA((count,)),
+            pltpu.SemaphoreType.DMA((count,)),
+            pltpu.SemaphoreType.DMA((count,)),
+            pltpu.SemaphoreType.DMA((count,)),
+        ],
+        compiler_params=pltpu.CompilerParams(collective_id=2, has_side_effects=True),
+        name="update_masters",
+    )(sums, own)
 
 
 def per_device(
@@ -299,19 +509,19 @@
     consts = tables(TILE + 2 * HALO, kernel_spectra.shape[1], HALO, TILE)
     rows_place, rows_t, cols_place = placements()
     own = masters.reshape(stored, HALF, LANES)
-    table = lax.all_gather(own.astype(jnp.bfloat16), "col", axis=0, tiled=True)
+    n_row = lax.axis_size("row")
+    n_col = lax.axis_size("col")
+    table = gather_masters(own.astype(jnp.bfloat16), n_col)
     shading, mask = image(
         inst_master, inst_orient, owner_map, table, tile_free, rows_place, cols_place, True
     )
-    padded = padded_2(mask, (("row", 0), ("col", 1)), HALO)
+    padded = with_halo(mask, n_row, n_col)
     resist, new_free, sums = tile_steps(
         inst_master, inst_orient, owner_map, socs_weights, padded, target, shading, tile_free,
         kernel_spectra, consts, rows_t, cols_place, total,
     )
-    part = lax.psum_scatter(sums, "col", scatter_dimension=0, tiled=True)
-    summed = lax.psum(part, "row").astype(jnp.float32)
-    fresh = smooth_packed(own - step_master * summed).astype(jnp.bfloat16)
-    table = lax.all_gather(fresh, "col", axis=0, tiled=True)
+    table = update_masters(sums, own, n_row, n_col)
+    fresh = lax.dynamic_slice_in_dim(table, lax.axis_index("col") * stored, stored, 0)
     (new_mask,) = image(
         inst_master, inst_orient, owner_map, table, new_free, rows_place, cols_place, False
     )

time: 364 us -> 214 us (0.59)
  waiting for transfers between devices: 196 us -> 0 us
  Pallas kernels: 134 us -> 207 us
  between operations: 13.9 us -> 0.68 us
  local copies, waits for them, and re-layouts: 10 us -> 1.87 us
  starting transfers between devices: 6.51 us -> 0 us
    pallas_call x0 -> x3, Pallas kernels: none -> 104 us  [the longest x1 53.3 us: update_masters(): pl.pallas_call(functools.partial(update_kernel, n_row, n_col), in_specs=[...]
    all_gather x2 -> x0, waiting for transfers between devices: 83.5 us -> none  [the longest x1 44.7 us: per_device(): table = lax.all_gather(own.astype(jnp.bfloat16), 'col', axis=0, tiled=True)]
    reduce_scatter x1 -> x0, waiting for transfers between devices: 69 us -> none  [per_device(): part = lax.psum_scatter(sums, 'col', scatter_dimension=0, tiled=True)]
    psum x1 -> x0, waiting for transfers between devices: 33 us -> none  [per_device(): summed = lax.psum(part, 'row').astype(jnp.float32)]
    pallas_call x1, Pallas kernels: 104 us -> 73.5 us  [tile_steps(): pl.pallas_call(tile_kernel, grid_spec=pltpu.PrefetchScalarGridSpec(num_sc...]
    ppermute x4 -> x0, waiting for transfers between devices: 10 us -> none  [the longest x2 6.53 us: padded_2(): after = lax.ppermute(initial, axis, down)]
    ppermute x4 -> x0, starting transfers between devices: 6.35 us -> none  [the longest x2 3.77 us: padded_2(): before = lax.ppermute(last, axis, up)]
    concatenate x2 -> x0, local copies, waits for them, and re-layouts: 4.02 us -> none  [padded_2(): value = jnp.concatenate([before, value, after], axis=dim)]
  transfers between devices with their start and end apart: 8 -> 0, of which waited for: 7 -> 0; matrix products, arithmetic and copies ran while one was open for 1% -> 0% of each run, Pallas kernels for 0% -> 0%
where the time goes in v2:
time: 214 us; the launch traced here: 211 us
  Pallas kernels  207 us (97%)
    pallas_call x1, Pallas kernels, tile_steps(): pl.pallas_call(tile_kernel, grid_spec=pltpu.PrefetchScalarGridSpec(num_sc...  73.5 us
    pallas_call x1, Pallas kernels, update_masters(): pl.pallas_call(functools.partial(update_kernel, n_row, n_col), in_specs=[...  53.3 us
    pallas_call x2, Pallas kernels, image(): pl.pallas_call(functools.partial(image_kernel, emit_mask), grid_spec=pltp...  29.9 us
    pallas_call x1, Pallas kernels, with_halo(): pl.pallas_call(functools.partial(halo_kernel, n_row, n_col), in_specs=[VM...  25.5 us
    pallas_call x1, Pallas kernels, gather_masters(): pl.pallas_call(functools.partial(gather_kernel, n_col), in_specs=[VM], ou...  24.9 us

profile of v2, /device:TPU:0, one launch (start us, length us, event | category | flops | bytes accessed | tf_op | source)
XLA Modules:
  0.0 211.4 jit_solution(13674005360878607238)
XLA Ops:
  0.6 1.0 copy.20
  1.6 0.0 copy-start
  1.6 0.7 bitcast_convert_fusion.own_ref
  2.4 24.9 %gather_masters.1.table_ref = bf16[128,32,128]{2,1,0:T(8,128)(2,1)} custom-call(bf16[16,32,128]{2,1,0:T(8,128)(2,1)} %bitcast_convert_fusion.own_ref), custom_call_target="tpu_custom_call" | custom-call | tf_op jit(solution)/shard_map/gather_masters/pallas_call | solution.py:311
  27.3 15.2 %image.2 = (f32[1024,1024]{1,0:T(8,128)}, bf16[1024,1024]{1,0:T(8,128)(2,1)}) custom-call(s32[16,16]{1,0:T(8,128)} %inst_ref.5, s32[16,16]{1,0:T(8,128)} %orient_ref.5, s32[128]{0:T(128)} %owner_ref.5, bf16[128,32,128]{2,1,0:T(8,128)(2,1)} %gather_masters.1.table_ref, f32[1024,1024]{1,0:T(8,128)} %free_ref.3, bf16[4,64,128]{2,1,0:T(8,128)(2,1)} %constant.34.clone.rows_ref, ...), custom_call_target="tpu_custom_call" | custom-call | tf_op jit(solution)/shard_map/image/pallas_call | solution.py:115
  42.4 25.5 %with_halo.1.padded_ref = bf16[1152,1280]{1,0:T(8,128)(2,1)} custom-call(bf16[1024,1024]{1,0:T(8,128)(2,1)} %get-tuple-element.8.mask_ref), custom_call_target="tpu_custom_call" | custom-call | tf_op jit(solution)/shard_map/with_halo/pallas_call | solution.py:376
  68.0 0.0 copy-done
  68.0 73.5 %tile_steps.1 = (f32[1024,1024]{1,0:T(8,128)}, f32[1024,1024]{1,0:T(8,128)}, bf16[128,32,128]{2,1,0:T(8,128)(2,1)}) custom-call(s32[16,16]{1,0:T(8,128)} %inst_ref.5, s32[16,16]{1,0:T(8,128)} %orient_ref.5, s32[128]{0:T(128)} %owner_ref.5, f32[8]{0:T(128)} %weights_ref.1, bf16[1152,1280]{1,0:T(8,128)(2,1)} %with_halo.1.padded_ref, f32[1024,1024]{1,0:T(8,128)} %target_ref.1, ...), custom_call_target="tpu_custom_call" | custom-call | tf_op jit(solution)/shard_map/tile_steps/pallas_call | solution.py:245
  141.5 53.3 %update_masters.1.table_ref = bf16[128,32,128]{2,1,0:T(8,128)(2,1)} custom-call(bf16[128,32,128]{2,1,0:T(8,128)(2,1)} %get-tuple-element.11.sums_ref, f32[16,32,128]{2,1,0:T(8,128)} %bitcast.7), custom_call_target="tpu_custom_call" | custom-call | tf_op jit(solution)/shard_map/update_masters/pallas_call | solution.py:486
  194.8 14.8 %image.3 = f32[1024,1024]{1,0:T(8,128)} custom-call(s32[16,16]{1,0:T(8,128)} %inst_ref.5, s32[16,16]{1,0:T(8,128)} %orient_ref.5, s32[128]{0:T(128)} %owner_ref.5, bf16[128,32,128]{2,1,0:T(8,128)(2,1)} %update_masters.1.table_ref, f32[1024,1024]{1,0:T(8,128)} %get-tuple-element.12.free_ref, bf16[4,64,128]{2,1,0:T(8,128)(2,1)} %constant.34.clone.rows_ref, ...), custom_call_target="tpu_custom_call" | custom-call | tf_op jit(solution)/shard_map/image/pallas_call | solution.py:115
  209.6 0.9 dynamic-slice_convert_fusion
  210.5 0.9 copy.23
Async XLA Ops:
  1.6 66.4 %copy-start = (f32[2,8,32,128]{3,2,1,0:T(8,128)}, f32[2,8,32,128]{3,2,1,0:T(8,128)S(1)}, u32[]{:S(2)}) copy-start(f32[2,8,32,128]{3,2,1,0:T(8,128)S(1)} %copy.20) | copy-start | bytes 786436

commit v3 on v2

--- a/solution.py
+++ b/solution.py
@@ -15,7 +15,7 @@
 CELL = 64
 LANES = 128
 HALF = CELL // 2
-BLOCK = 256
+BLOCK = 512
 
 step_free = 1.0
 step_master = 0.05
@@ -99,6 +99,13 @@
         outs[0][:, lanes] = value
         if emit_mask:
             outs[1][:, lanes] = value.astype(jnp.bfloat16)
+            left = left_mask(HALF)
+            if pair == 0:
+                turned = pltpu.roll(value[HALF:], CELL, 1)
+                outs[2][...] = jnp.where(left, value[:HALF], turned).astype(jnp.bfloat16)
+            if pair == free_ref.shape[1] // LANES - 1:
+                turned = pltpu.roll(value[:HALF], CELL, 1)
+                outs[3][...] = jnp.where(left, turned, value[HALF:]).astype(jnp.bfloat16)
 
 
 def whole_spec(array):
@@ -110,15 +117,19 @@
     height, width = free.shape
     strip = pl.BlockSpec((CELL, width), lambda a, *_: (a, 0))
     out_shape = [jax.ShapeDtypeStruct(free.shape, jnp.float32)]
+    out_specs = [strip]
     if emit_mask:
-        out_shape.append(jax.ShapeDtypeStruct(free.shape, jnp.bfloat16))
+        edge = jax.ShapeDtypeStruct((height // 2, LANES), jnp.bfloat16)
+        edge_spec = pl.BlockSpec((HALF, LANES), lambda a, *_: (a, 0))
+        out_shape += [jax.ShapeDtypeStruct(free.shape, jnp.bfloat16), edge, edge]
+        out_specs += [strip, edge_spec, edge_spec]
     return pl.pallas_call(
         functools.partial(image_kernel, emit_mask),
         grid_spec=pltpu.PrefetchScalarGridSpec(
             num_scalar_prefetch=3,
             grid=(height // CELL,),
             in_specs=[whole_spec(table), strip, whole_spec(rows_place), whole_spec(cols_place)],
-            out_specs=[strip] * len(out_shape),
+            out_specs=out_specs,
         ),
         out_shape=out_shape,
         name="image",
@@ -283,105 +294,202 @@
     pl.semaphore_wait(barrier, len(peers))
 
 
-def gather_kernel(n_col, own_ref, table_ref, send_sem, recv_sem):
+def level_peers(n_row, n_col):
+    r = lax.axis_index("row")
+    c = lax.axis_index("col")
+    long = n_col // 2
+    z, y = lax.div(c, 2), lax.rem(c, 2)
+    x, core = lax.div(r, 2), lax.rem(r, 2)
+    p = x * 2 + y
+
+    def z_at(t):
+        return lax.rem(z + t + long, long)
+
+    def p_at(t):
+        q = lax.rem(p + t + n_row, n_row)
+        return lax.div(q, 2), lax.rem(q, 2)
+
+    return r, c, z, y, x, core, long, z_at, p_at
+
+
+def gather_ids(n_row, n_col):
+    r, c, z, y, x, core, long, z_at, p_at = level_peers(n_row, n_col)
+    ids = [(r, z_at(t) * 2 + y) for t in range(1, long)]
+    for t in range(1, n_row):
+        px, py = p_at(t)
+        ids.append((px * 2 + core, z * 2 + py))
+    return ids + [(x * 2 + 1 - core, c)]
+
+
+def gather_levels(n_row, n_col, own, table_ref, stored, send_sem, recv_sem):
+    r, c, z, y, x, core, long, z_at, p_at = level_peers(n_row, n_col)
+    share = stored // n_row
+
+    def block(row, col):
+        return table_ref.at[pl.ds(col * stored + row * share, share)]
+
+    def make(src, dst, level, at, peer):
+        return pltpu.make_async_remote_copy(
+            src_ref=src,
+            dst_ref=dst,
+            send_sem=send_sem.at[level, at],
+            recv_sem=recv_sem.at[level, at],
+            device_id=peer,
+            device_id_type=MESH,
+        )
+
+    partner = (x * 2 + 1 - core, c)
+    mine = block(r, c)
+    first = [make(own, mine, 0, t, (r, z_at(t) * 2 + y)) for t in range(1, long)]
+    for copy in first:
+        copy.start()
+    second = []
+    third = []
+    for t in range(long):
+        if t > 0:
+            first[t - 1].wait_recv()
+        here = block(r, z_at(-t) * 2 + y)
+        src = own if t == 0 else here
+        for q in range(1, n_row):
+            px, py = p_at(q)
+            copy = make(src, here, 1, t * n_row + q, (px * 2 + core, z * 2 + py))
+            copy.start()
+            second.append(copy)
+        copy = make(src, here, 2, t * n_row, partner)
+        copy.start()
+        third.append(copy)
+    for t in range(long):
+        for q in range(1, n_row):
+            second[t * (n_row - 1) + q - 1].wait_recv()
+            px, py = p_at(-q)
+            here = block(px * 2 + core, z_at(-t) * 2 + py)
+            copy = make(here, here, 2, t * n_row + q, partner)
+            copy.start()
+            third.append(copy)
+    for copy in third:
+        copy.wait_recv()
+    for copy in first + second + third:
+        copy.wait_send()
+
+
+def gather_sems(n_row, n_col):
+    shape = (3, n_row * n_col // 2)
+    return [pltpu.SemaphoreType.DMA(shape), pltpu.SemaphoreType.DMA(shape)]
+
+
+def gather_kernel(n_row, n_col, own_ref, table_ref, send_sem, recv_sem):
     r = lax.axis_index("row")
     c = lax.axis_index("col")
     stored = own_ref.shape[0]
-    greet([(r, lax.rem(c + t, n_col)) for t in range(1, n_col)])
-    here = table_ref.at[pl.ds(c * stored, stored)]
-    copies = [
-        pltpu.make_async_remote_copy(
-            src_ref=own_ref,
-            dst_ref=here,
-            send_sem=send_sem.at[t],
-            recv_sem=recv_sem.at[t],
-            device_id=(r, lax.rem(c + t, n_col)),
-            device_id_type=MESH,
-        )
-        for t in range(1, n_col)
-    ]
-    for copy in copies:
-        copy.start()
-    table_ref[pl.ds(c * stored, stored)] = own_ref[...]
-    for copy in copies:
-        copy.wait()
-
-
-def gather_masters(own, n_col):
+    share = stored // n_row
+    greet(gather_ids(n_row, n_col))
+    own = own_ref.at[pl.ds(r * share, share)]
+    table_ref[pl.ds(c * stored + r * share, share)] = own_ref[pl.ds(r * share, share)]
+    gather_levels(n_row, n_col, own, table_ref, stored, send_sem, recv_sem)
+
+
+def gather_masters(own, n_row, n_col):
     return pl.pallas_call(
-        functools.partial(gather_kernel, n_col),
+        functools.partial(gather_kernel, n_row, n_col),
         in_specs=[VM],
         out_specs=VM,
         out_shape=jax.ShapeDtypeStruct((n_col * own.shape[0],) + own.shape[1:], own.dtype),
-        scratch_shapes=[pltpu.SemaphoreType.DMA((n_col,)), pltpu.SemaphoreType.DMA((n_col,))],
+        scratch_shapes=gather_sems(n_row, n_col),
         compiler_params=pltpu.CompilerParams(collective_id=0, has_side_effects=True),
         name="gather_masters",
     )(own)
 
 
-def halo_kernel(n_row, n_col, mask_ref, out_ref, send_sem, recv_sem):
+def halo_kernel(
+    n_row, n_col, mask_ref, edge_l_ref, edge_r_ref, out_ref, from_l, from_r, send_sem, recv_sem
+):
     r = lax.axis_index("row")
     c = lax.axis_index("col")
     height, width = mask_ref.shape
+    packed = height // 2
+    middle = slice(LANES, LANES + width)
     row_parts = {
         -1: (slice(0, HALO), slice(HALO + height, 2 * HALO + height)),
-        0: (slice(0, height), slice(HALO, HALO + height)),
         1: (slice(height - HALO, height), slice(0, HALO)),
     }
-    col_parts = {
-        -1: (slice(0, LANES), slice(LANES + width, 2 * LANES + width)),
-        0: (slice(0, width), slice(LANES, LANES + width)),
-        1: (slice(width - LANES, width), slice(0, LANES)),
+    edge_parts = {
+        -1: (slice(0, HALF), slice(HALF + packed, 2 * HALF + packed)),
+        0: (slice(0, packed), slice(HALF, HALF + packed)),
+        1: (slice(packed - HALF, packed), slice(0, HALF)),
     }
     moves = [(0, 1), (0, -1), (1, 0), (-1, 0), (1, 1), (1, -1), (-1, 1), (-1, -1)]
     ids = [(lax.rem(r + n_row + dr, n_row), lax.rem(c + n_col + dc, n_col)) for dr, dc in moves]
-    greet(ids)
-    copies = []
+
+    def inside(dr, dc):
+        return (r + dr >= 0) & (r + dr < n_row) & (c + dc >= 0) & (c + dc < n_col)
+
+    work = []
     for at, (dr, dc) in enumerate(moves):
-        src_rows, dst_rows = row_parts[dr]
-        src_cols, dst_cols = col_parts[dc]
+        if dc == 0:
+            src, dst = row_parts[dr]
+            src, dst = mask_ref.at[src], out_ref.at[dst, middle]
+        else:
+            src, dst = edge_parts[dr]
+            src = (edge_r_ref if dc == 1 else edge_l_ref).at[src]
+            dst = (from_l if dc == 1 else from_r).at[dst]
         copy = pltpu.make_async_remote_copy(
-            src_ref=mask_ref.at[src_rows, src_cols],
-            dst_ref=out_ref.at[dst_rows, dst_cols],
+            src_ref=src,
+            dst_ref=dst,
             send_sem=send_sem.at[at],
             recv_sem=recv_sem.at[at],
             device_id=ids[at],
             device_id_type=MESH,
         )
-        copy.start()
-        copies.append(copy)
-    out_ref[HALO : HALO + height, LANES : LANES + width] = mask_ref[...]
-    for copy in copies:
-        copy.wait()
-
-    @pl.when(r == 0)
-    def _():
-        out_ref[:HALO, :] = jnp.zeros((HALO, width + 2 * LANES), out_ref.dtype)
-
-    @pl.when(r == n_row - 1)
-    def _():
-        out_ref[HALO + height :, :] = jnp.zeros((HALO, width + 2 * LANES), out_ref.dtype)
-
-    @pl.when(c == 0)
-    def _():
-        out_ref[:, :LANES] = jnp.zeros((height + 2 * HALO, LANES), out_ref.dtype)
-
-    @pl.when(c == n_col - 1)
-    def _():
-        out_ref[:, LANES + width :] = jnp.zeros((height + 2 * HALO, LANES), out_ref.dtype)
-
-
-def with_halo(mask, n_row, n_col):
+        work.append((copy, dst, inside(dr, dc), inside(-dr, -dc)))
+    greet(ids)
+    for copy, dst, sends, gets in work:
+        pl.when(sends)(copy.start)
+    for copy, dst, sends, gets in work:
+
+        @pl.when(jnp.logical_not(gets))
+        def _():
+            dst[...] = jnp.zeros(dst.shape, dst.dtype)
+
+    out_ref[HALO : HALO + height, middle] = mask_ref[...]
+    for copy, dst, sends, gets in work:
+        pl.when(gets)(copy.wait_recv)
+    left = left_mask(HALF)
+
+    def unpack(a, carry):
+        rows = pl.ds(pl.multiple_of(a * HALF, HALF), HALF)
+        upper = pl.ds(pl.multiple_of(a * CELL, CELL), HALF)
+        lower = pl.ds(pl.multiple_of(a * CELL + HALF, HALF), HALF)
+        one = from_l[rows].astype(jnp.float32)
+        two = from_r[rows].astype(jnp.float32)
+        cast = lambda v: v.astype(jnp.bfloat16)
+        last = slice(LANES + width, 2 * LANES + width)
+        out_ref[upper, :LANES] = cast(jnp.where(left, 0.0, pltpu.roll(one, CELL, 1)))
+        out_ref[lower, :LANES] = cast(jnp.where(left, 0.0, one))
+        out_ref[upper, last] = cast(jnp.where(left, two, 0.0))
+        out_ref[lower, last] = cast(jnp.where(left, pltpu.roll(two, CELL, 1), 0.0))
+        return carry
+
+    lax.fori_loop(0, (height + 2 * HALO) // CELL, unpack, 0)
+    for copy, dst, sends, gets in work:
+        pl.when(sends)(copy.wait_send)
+
+
+def with_halo(mask, edge_l, edge_r, n_row, n_col):
     height, width = mask.shape
     return pl.pallas_call(
         functools.partial(halo_kernel, n_row, n_col),
-        in_specs=[VM],
+        in_specs=[VM, VM, VM],
         out_specs=VM,
         out_shape=jax.ShapeDtypeStruct((height + 2 * HALO, width + 2 * LANES), mask.dtype),
-        scratch_shapes=[pltpu.SemaphoreType.DMA((8,)), pltpu.SemaphoreType.DMA((8,))],
+        scratch_shapes=[
+            pltpu.VMEM((height // 2 + 2 * HALF, LANES), mask.dtype),
+            pltpu.VMEM((height // 2 + 2 * HALF, LANES), mask.dtype),
+            pltpu.SemaphoreType.DMA((8,)),
+            pltpu.SemaphoreType.DMA((8,)),
+        ],
         compiler_params=pltpu.CompilerParams(collective_id=1, has_side_effects=True),
         name="with_halo",
-    )(mask)
+    )(mask, edge_l, edge_r)
 
 
 def smooth_packed(cells):
@@ -458,26 +566,7 @@
 
     lax.fori_loop(1, count, end_part, 0)
 
-    def fresh_copy(t):
-        return pltpu.make_async_remote_copy(
-            src_ref=fresh,
-            dst_ref=table_ref.at[pl.ds(mine, share)],
-            send_sem=send2_sem.at[t],
-            recv_sem=recv2_sem.at[t],
-            device_id=split_id(lax.rem(me + t, count), n_col),
-            device_id_type=MESH,
-        )
-
-    def start_fresh(t, carry):
-        fresh_copy(t).start()
-        return carry
-
-    def end_fresh(t, carry):
-        fresh_copy(t).wait()
-        return carry
-
-    lax.fori_loop(1, count, start_fresh, 0)
-    lax.fori_loop(1, count, end_fresh, 0)
+    gather_levels(n_row, n_col, fresh, table_ref, stored, send2_sem, recv2_sem)
 
 
 def update_masters(sums, own, n_row, n_col):
@@ -493,8 +582,7 @@
             pltpu.VMEM(piece, jnp.bfloat16),
             pltpu.SemaphoreType.DMA((count,)),
             pltpu.SemaphoreType.DMA((count,)),
-            pltpu.SemaphoreType.DMA((count,)),
-            pltpu.SemaphoreType.DMA((count,)),
+            *gather_sems(n_row, n_col),
         ],
         compiler_params=pltpu.CompilerParams(collective_id=2, has_side_effects=True),
         name="update_masters",
@@ -511,11 +599,11 @@
     own = masters.reshape(stored, HALF, LANES)
     n_row = lax.axis_size("row")
     n_col = lax.axis_size("col")
-    table = gather_masters(own.astype(jnp.bfloat16), n_col)
-    shading, mask = image(
+    table = gather_masters(own.astype(jnp.bfloat16), n_row, n_col)
+    shading, mask, edge_l, edge_r = image(
         inst_master, inst_orient, owner_map, table, tile_free, rows_place, cols_place, True
     )
-    padded = with_halo(mask, n_row, n_col)
+    padded = with_halo(mask, edge_l, edge_r, n_row, n_col)
     resist, new_free, sums = tile_steps(
         inst_master, inst_orient, owner_map, socs_weights, padded, target, shading, tile_free,
         kernel_spectra, consts, rows_t, cols_place, total,

time: 214 us -> 182 us (0.85)
  Pallas kernels: 207 us -> 177 us
    pallas_call x1, Pallas kernels: 25.5 us -> 13.2 us  [with_halo(): pl.pallas_call(functools.partial(halo_kernel, n_row, n_col), in_specs=[VM...]
    pallas_call x1, Pallas kernels: 53.3 us -> 44.7 us  [update_masters(): pl.pallas_call(functools.partial(update_kernel, n_row, n_col), in_specs=[...]
    pallas_call x1, Pallas kernels: 24.9 us -> 17.5 us  [gather_masters(): pl.pallas_call(functools.partial(gather_kernel, n_row, n_col), in_specs=[...]
    pallas_call x1, Pallas kernels: 73.5 us -> 71.1 us  [tile_steps(): pl.pallas_call(tile_kernel, grid_spec=pltpu.PrefetchScalarGridSpec(num_sc...]
where the time goes in v3:
time: 182 us; the launch traced here: 181 us
  Pallas kernels  177 us (97%)
  local copies, waits for them, and re-layouts  1.87 us (1%)
    pallas_call x1, Pallas kernels, tile_steps(): pl.pallas_call(tile_kernel, grid_spec=pltpu.PrefetchScalarGridSpec(num_sc...  71.1 us
    pallas_call x1, Pallas kernels, update_masters(): pl.pallas_call(functools.partial(update_kernel, n_row, n_col), in_specs=[...  44.7 us
    pallas_call x2, Pallas kernels, image(): pl.pallas_call(functools.partial(image_kernel, emit_mask), grid_spec=pltp...  30 us
    pallas_call x1, Pallas kernels, gather_masters(): pl.pallas_call(functools.partial(gather_kernel, n_row, n_col), in_specs=[...  17.5 us
    pallas_call x1, Pallas kernels, with_halo(): pl.pallas_call(functools.partial(halo_kernel, n_row, n_col), in_specs=[VM...  13.2 us

profile of v3, /device:TPU:0, one launch (start us, length us, event | category | flops | bytes accessed | tf_op | source)
XLA Modules:
  0.0 180.8 jit_solution(6561766693534998162)
XLA Ops:
  0.6 1.0 copy.20
  1.6 0.0 copy-start
  1.6 0.7 bitcast_convert_fusion.own_ref
  2.4 17.5 %gather_masters.1.table_ref = bf16[128,32,128]{2,1,0:T(8,128)(2,1)} custom-call(bf16[16,32,128]{2,1,0:T(8,128)(2,1)} %bitcast_convert_fusion.own_ref), custom_call_target="tpu_custom_call" | custom-call | tf_op jit(solution)/shard_map/gather_masters/pallas_call | solution.py:392
  19.9 15.2 %image.2 = (f32[1024,1024]{1,0:T(8,128)}, bf16[1024,1024]{1,0:T(8,128)(2,1)}, bf16[512,128]{1,0:T(8,128)(2,1)}, bf16[512,128]{1,0:T(8,128)(2,1)}) custom-call(s32[16,16]{1,0:T(8,128)} %inst_ref.5, s32[16,16]{1,0:T(8,128)} %orient_ref.5, s32[128]{0:T(128)} %owner_ref.5, bf16[128,32,128]{2,1,0:T(8,128)(2,1)} %gather_masters.1.table_ref, ...), custom_call_target="tpu_custom_call" | custom-call | tf_op jit(solution)/shard_map/image/pallas_call | solution.py:126
  35.1 13.2 %with_halo.1.padded_ref = bf16[1152,1280]{1,0:T(8,128)(2,1)} custom-call(bf16[1024,1024]{1,0:T(8,128)(2,1)} %get-tuple-element.10.mask_ref, bf16[512,128]{1,0:T(8,128)(2,1)} %get-tuple-element.11.edge_l_ref, bf16[512,128]{1,0:T(8,128)(2,1)} %get-tuple-element.12.edge_r_ref), custom_call_target="tpu_custom_call" | custom-call | tf_op jit(solution)/shard_map/with_halo/pallas_call | solution.py:479
  48.3 0.0 copy-done
  48.3 71.1 %tile_steps.1 = (f32[1024,1024]{1,0:T(8,128)}, f32[1024,1024]{1,0:T(8,128)}, bf16[128,32,128]{2,1,0:T(8,128)(2,1)}) custom-call(s32[16,16]{1,0:T(8,128)} %inst_ref.5, s32[16,16]{1,0:T(8,128)} %orient_ref.5, s32[128]{0:T(128)} %owner_ref.5, f32[8]{0:T(128)} %weights_ref.1, bf16[1152,1280]{1,0:T(8,128)(2,1)} %with_halo.1.padded_ref, f32[1024,1024]{1,0:T(8,128)} %target_ref.1, ...), custom_call_target="tpu_custom_call" | custom-call | tf_op jit(solution)/shard_map/tile_steps/pallas_call | solution.py:256
  119.5 44.7 %update_masters.1.table_ref = bf16[128,32,128]{2,1,0:T(8,128)(2,1)} custom-call(bf16[128,32,128]{2,1,0:T(8,128)(2,1)} %get-tuple-element.15.sums_ref, f32[16,32,128]{2,1,0:T(8,128)} %bitcast.7), custom_call_target="tpu_custom_call" | custom-call | tf_op jit(solution)/shard_map/update_masters/pallas_call | solution.py:575
  164.2 14.8 %image.3 = f32[1024,1024]{1,0:T(8,128)} custom-call(s32[16,16]{1,0:T(8,128)} %inst_ref.5, s32[16,16]{1,0:T(8,128)} %orient_ref.5, s32[128]{0:T(128)} %owner_ref.5, bf16[128,32,128]{2,1,0:T(8,128)(2,1)} %update_masters.1.table_ref, f32[1024,1024]{1,0:T(8,128)} %get-tuple-element.16.free_ref, bf16[4,64,128]{2,1,0:T(8,128)(2,1)} %constant.34.clone.rows_ref, ...), custom_call_target="tpu_custom_call" | custom-call | tf_op jit(solution)/shard_map/image/pallas_call | solution.py:126
  179.0 0.9 dynamic-slice_convert_fusion
  179.9 0.9 copy.23
Async XLA Ops:
  1.6 46.7 %copy-start = (f32[2,8,32,128]{3,2,1,0:T(8,128)}, f32[2,8,32,128]{3,2,1,0:T(8,128)S(1)}, u32[]{:S(2)}) copy-start(f32[2,8,32,128]{3,2,1,0:T(8,128)S(1)} %copy.20) | copy-start | bytes 786436
